TPU v7x, 256 devices: a whole 4x4x8 slice. The times are simulated.
256 devices in a mesh: lat: 16 (over z, x_lo), lon: 16 (over x_hi, y, core).
Axes of the slice: x: 4 (x_hi: 2, x_lo: 2; x = x_hi * 2 + x_lo), y: 4, z: 8, core: 2. Of those that a mesh axis runs over, the one named last changes fastest.
Arguments:
- tokens: bfloat16 [128, 256, 2, 1024], P('lat', 'lon'), may hold values from -6 to 6
- norm_gain: bfloat16 [1024], replicated, may hold values from 0.099609375 to 1.8984375
- q_weight: bfloat16 [1024, 1024], replicated, may hold values from -3 to 3
- k_weight: bfloat16 [1024, 1024], replicated, may hold values from -3 to 3
- v_weight: bfloat16 [1024, 1024], replicated, may hold values from -0.1875 to 0.1875
- o_weight: bfloat16 [1024, 1024], replicated, may hold values from -0.75 to 0.75
- band_start: int32 [16], replicated, may hold values from -15 to 0, as said below
- band_width: int32 [16], replicated, may hold values from 2 to 16, as said below
Outputs:
- mixed: bfloat16 [128, 256, 2, 1024], P('lat', 'lon')
Inputs may be any that keep to these rules, and one draw needn't show every extreme that they name: `band_width`: band 0 and band 16 - 1 have width 16; widths need not grow band by band. 1 - band_width[b] <= band_start[b], so a query's own block is always seen.
All inputs are finite; a program needn't handle non-finite values.
Results may differ from a plain program's by a relative error of at most 0.006.
Values may be sent and summed in bfloat16 or wider, within the bound.
No kernel may reach another device: no remote copies, remote signals or barrier semaphores. Data moves between devices by JAX's collectives and lax.ppermute only.
A program may use at most 128 MiB of HBM per device.

v0:
```python
import jax
import jax.numpy as jnp
from jax import lax
from jax.sharding import PartitionSpec as P

HD = 64


def with_halo(array, sides, width):
    for axis, dim in sides:
        devices, length = (lax.axis_size(axis), array.shape[dim])
        up = [(i, (i + 1) % devices) for i in range(devices - 1)]
        down = [(j, i) for i, j in up]
        last = lax.slice_in_dim(array, length - width, length, axis=dim)
        leading = lax.slice_in_dim(array, 0, width, axis=dim)
        before = lax.ppermute(last, axis, up)
        after = lax.ppermute(leading, axis, down)
        array = jnp.concatenate([before, array, after], axis=dim)
    return array


def from_behind(value, axis, steps):
    count = lax.axis_size(axis)
    pairs = [(source, (source + steps) % count) for source in range(count)]
    return lax.ppermute(value, axis, pairs)


def body(tokens, norm_gain, q_weight, k_weight, v_weight, o_weight, band_start, band_width):
    rows, columns, levels, width = tokens.shape
    heads = width // HD
    n_lon = lax.axis_size("lon")
    n_lat = lax.axis_size("lat")
    band = lax.axis_index("lat")
    block = lax.axis_index("lon")
    wide = tokens.astype(jnp.float32)
    normed = (
        wide
        * lax.rsqrt(jnp.mean(wide * wide, -1, keepdims=True) + 1e-06)
        * norm_gain.astype(jnp.float32)
    ).astype(jnp.bfloat16)
    flat = normed.reshape(-1, width)
    query = jnp.dot(flat, q_weight, preferred_element_type=jnp.float32).astype(jnp.bfloat16)
    keys = jnp.dot(flat, k_weight, preferred_element_type=jnp.float32).astype(jnp.bfloat16)
    values = jnp.dot(flat, v_weight, preferred_element_type=jnp.float32).astype(jnp.bfloat16)
    query_heads = query.reshape(-1, heads, HD)
    count_queries = query_heads.shape[0]
    pair = jnp.stack(
        [keys.reshape(rows, columns, levels, width), values.reshape(rows, columns, levels, width)]
    )
    padded = with_halo(pair, (("lat", 1),), 1)
    edges = jnp.stack([pair[:, 0], pair[:, rows - 1]], axis=1)
    across = from_behind(edges, "lon", n_lon // 2)
    top_row = across[:, 0]
    bottom_row = across[:, 1]
    first = jnp.where(band == 0, top_row, padded[:, 0])
    last = jnp.where(band == n_lat - 1, bottom_row, padded[:, rows + 1])
    extended = jnp.concatenate([first[:, None], padded[:, 1 : rows + 1], last[:, None]], axis=1)
    start_here = band_start[band]
    span_here = band_width[band]
    scale = HD ** (-0.5)

    def attend(state, piece, owner):
        inside = jnp.mod(owner - block - start_here, n_lon) < span_here

        def update(carry):
            top, total, weighted = carry
            key_heads = piece[0].reshape(-1, heads, HD)
            value_heads = piece[1].reshape(-1, heads, HD)
            scores = (
                jnp.einsum(
                    "qhd,khd->hqk", query_heads, key_heads, preferred_element_type=jnp.float32
                )
                * scale
            )
            new_top = jnp.maximum(top, jnp.max(scores, -1))
            raw = jnp.exp(scores - new_top[..., None])
            fade = jnp.exp(top - new_top)
            total = total * fade + jnp.sum(raw, -1)
            weighted = weighted * fade[..., None] + jnp.einsum(
                "hqk,khd->hqd",
                raw.astype(jnp.bfloat16),
                value_heads,
                preferred_element_type=jnp.float32,
            )
            return (new_top, total, weighted)

        def keep(carry):
            return carry

        return lax.cond(inside, update, keep, state)

    initial = (
        jnp.full((heads, count_queries), -1e30, jnp.float32),
        jnp.zeros((heads, count_queries), jnp.float32),
        jnp.zeros((heads, count_queries, HD), jnp.float32),
    )
    carry = initial
    piece = lax.all_gather(extended, "lon", axis=2, tiled=True)
    count = piece.shape[2] // columns
    split = jnp.moveaxis(piece.reshape(2, rows + 2, count, columns, levels, width), 2, 0)

    def advance(inner, element):
        single, offset = element
        return (attend(inner, single, offset), None)

    carry, unused = lax.scan(advance, carry, (split, jnp.arange(count, dtype=jnp.int32)))
    state = carry
    top, total, weighted = state
    attended = (
        (weighted / total[..., None]).transpose(1, 0, 2).reshape(-1, width).astype(jnp.bfloat16)
    )
    mixed = wide.reshape(-1, width) + jnp.dot(
        attended, o_weight, preferred_element_type=jnp.float32
    )
    return mixed.astype(jnp.bfloat16).reshape(rows, columns, levels, width)


def solution(mesh):
    placed = (P("lat", "lon", None, None), P(), P(), P(), P(), P(), P(), P())
    return jax.shard_map(
        body, mesh=mesh, in_specs=placed, out_specs=P("lat", "lon", None, None), check_vma=False
    )
```

profile of v0, /device:TPU:1, one launch (start us, length us, event | category | flops | bytes accessed | tf_op | source)
XLA Modules:
  0.0 453.6 jit_solution(10605950701415543880)
XLA Ops:
  14.9 3.6 collective-permute-start
  22.3 4.1 collective-permute-done.1
  33.7 134.1 %all-gather.2.cloned.1.call-done = bf16[2,10,256,2,1024]{4,2,3,1,0:T(8,128)(2,1)} async-done(((bf16[2,10,16,2,1024]{4,2,3,1,0:T(8,128)(2,1)}), bf16[2,10,256,2,1024]{4,2,3,1,0:T(8,128)(2,1)}) %all-gather.2.cloned.1.call-update) | async-done | bytes 20971536 | tf_op jit(solution)/shard_map/all_gather | solution.py:98
  167.8 38.5 %copy.30 = bf16[16,2,10,16,2,1024]{5,4,3,2,1,0:T(2,128)(2,1)} copy(bf16[16,2,10,16,2,1024]{5,3,0,4,2,1:T(8,128)(2,1)} %bitcast.33) | data formatting | bytes 41943040 | tf_op jit(solution)/shard_map/while | solution.py:106
  207.4 234.3 %while.16 = (s32[]{:T(128)}, f32[16,256]{1,0:T(8,128)S(1)}, f32[16,256]{1,0:T(8,128)S(1)}, f32[16,256,64]{1,2,0:T(8,128)}, s32[16]{0:T(128)S(1)}, /*index=5*/s32...) while((s32[]{:T(128)}, f32[16,256]{1,0:T(8,128)S(1)}, ...), condition=%wide.region_6.7_spmd, body=%wide.region_1.6_spmd.sunk | while | flops 346562560 | bytes 46137788 | solution.py:106
  209.8 12.3 %conditional.2 = ((f32[16,256]{1,0:T(8,128)S(1)}, f32[16,256]{1,0:T(8,128)S(1)}, f32[16,256,64]{1,2,0:T(8,128)})) conditional(s32[]{:T(128)} %convert_element_type.63, (f32[16,256]{1,0:T(8,128)S(1)}, f32[16,256]{1,0:T(8,128)S(1)}, f32[16,256,64]{1,2,0:T(8,128)}) %tuple.46, (bf16[16,2,10,16,2,1024]{5,4,3,2,1,0:T(2,128)(2,1)}, s32[]{:T(128)}, ...), branch_computations={%region_2.2_spmd, %region_3.5_spmd} | conditional | flops 346562560 | bytes 46137424 | solution.py:90
  209.8 2.6 constant_dynamic-slice_fusion.1
  217.1 4.9 %fusion.7 = f32[16,256,64]{1,2,0:T(8,128)} fusion(f32[16,320,256]{2,1,0:T(8,128)} %copy-done.2, f32[16,256]{1,0:T(8,128)S(1)} %max.3, bf16[320,16,64]{2,1,0:T(8,128)(2,1)S(1)} %squeeze.25, f32[16,256,64]{1,2,0:T(8,128)} %get-tuple-element.163, f32[16,256]{1,0:T(8,128)S(1)} %get-tuple-element.243), kind=kOutput, calls=%fused_computation.8 | convolution fusion | flops 172228608 | bytes 8028160 | tf_op jit(solution)/shard_map/while/body/eval_jaxpr/cond/branch_1_fun/hqk,khd->hqd/dot_general | solution.py:79
  224.4 12.3 %conditional.2 = ((f32[16,256]{1,0:T(8,128)S(1)}, f32[16,256]{1,0:T(8,128)S(1)}, f32[16,256,64]{1,2,0:T(8,128)})) conditional(s32[]{:T(128)} %convert_element_type.63, (f32[16,256]{1,0:T(8,128)S(1)}, f32[16,256]{1,0:T(8,128)S(1)}, f32[16,256,64]{1,2,0:T(8,128)}) %tuple.46, (bf16[16,2,10,16,2,1024]{5,4,3,2,1,0:T(2,128)(2,1)}, s32[]{:T(128)}, ...), branch_computations={%region_2.2_spmd, %region_3.5_spmd} | conditional | flops 346562560 | bytes 46137424 | solution.py:90
  224.4 2.6 constant_dynamic-slice_fusion.1
  231.8 4.9 %fusion.7 = f32[16,256,64]{1,2,0:T(8,128)} fusion(f32[16,320,256]{2,1,0:T(8,128)} %copy-done.2, f32[16,256]{1,0:T(8,128)S(1)} %max.3, bf16[320,16,64]{2,1,0:T(8,128)(2,1)S(1)} %squeeze.25, f32[16,256,64]{1,2,0:T(8,128)} %get-tuple-element.163, f32[16,256]{1,0:T(8,128)S(1)} %get-tuple-element.243), kind=kOutput, calls=%fused_computation.8 | convolution fusion | flops 172228608 | bytes 8028160 | tf_op jit(solution)/shard_map/while/body/eval_jaxpr/cond/branch_1_fun/hqk,khd->hqd/dot_general | solution.py:79
  239.1 12.3 %conditional.2 = ((f32[16,256]{1,0:T(8,128)S(1)}, f32[16,256]{1,0:T(8,128)S(1)}, f32[16,256,64]{1,2,0:T(8,128)})) conditional(s32[]{:T(128)} %convert_element_type.63, (f32[16,256]{1,0:T(8,128)S(1)}, f32[16,256]{1,0:T(8,128)S(1)}, f32[16,256,64]{1,2,0:T(8,128)}) %tuple.46, (bf16[16,2,10,16,2,1024]{5,4,3,2,1,0:T(2,128)(2,1)}, s32[]{:T(128)}, ...), branch_computations={%region_2.2_spmd, %region_3.5_spmd} | conditional | flops 346562560 | bytes 46137424 | solution.py:90
  239.1 2.6 constant_dynamic-slice_fusion.1
  246.4 4.9 %fusion.7 = f32[16,256,64]{1,2,0:T(8,128)} fusion(f32[16,320,256]{2,1,0:T(8,128)} %copy-done.2, f32[16,256]{1,0:T(8,128)S(1)} %max.3, bf16[320,16,64]{2,1,0:T(8,128)(2,1)S(1)} %squeeze.25, f32[16,256,64]{1,2,0:T(8,128)} %get-tuple-element.163, f32[16,256]{1,0:T(8,128)S(1)} %get-tuple-element.243), kind=kOutput, calls=%fused_computation.8 | convolution fusion | flops 172228608 | bytes 8028160 | tf_op jit(solution)/shard_map/while/body/eval_jaxpr/cond/branch_1_fun/hqk,khd->hqd/dot_general | solution.py:79
  253.7 12.3 %conditional.2 = ((f32[16,256]{1,0:T(8,128)S(1)}, f32[16,256]{1,0:T(8,128)S(1)}, f32[16,256,64]{1,2,0:T(8,128)})) conditional(s32[]{:T(128)} %convert_element_type.63, (f32[16,256]{1,0:T(8,128)S(1)}, f32[16,256]{1,0:T(8,128)S(1)}, f32[16,256,64]{1,2,0:T(8,128)}) %tuple.46, (bf16[16,2,10,16,2,1024]{5,4,3,2,1,0:T(2,128)(2,1)}, s32[]{:T(128)}, ...), branch_computations={%region_2.2_spmd, %region_3.5_spmd} | conditional | flops 346562560 | bytes 46137424 | solution.py:90
  253.7 2.6 constant_dynamic-slice_fusion.1
  261.1 4.9 %fusion.7 = f32[16,256,64]{1,2,0:T(8,128)} fusion(f32[16,320,256]{2,1,0:T(8,128)} %copy-done.2, f32[16,256]{1,0:T(8,128)S(1)} %max.3, bf16[320,16,64]{2,1,0:T(8,128)(2,1)S(1)} %squeeze.25, f32[16,256,64]{1,2,0:T(8,128)} %get-tuple-element.163, f32[16,256]{1,0:T(8,128)S(1)} %get-tuple-element.243), kind=kOutput, calls=%fused_computation.8 | convolution fusion | flops 172228608 | bytes 8028160 | tf_op jit(solution)/shard_map/while/body/eval_jaxpr/cond/branch_1_fun/hqk,khd->hqd/dot_general | solution.py:79
  268.4 12.3 %conditional.2 = ((f32[16,256]{1,0:T(8,128)S(1)}, f32[16,256]{1,0:T(8,128)S(1)}, f32[16,256,64]{1,2,0:T(8,128)})) conditional(s32[]{:T(128)} %convert_element_type.63, (f32[16,256]{1,0:T(8,128)S(1)}, f32[16,256]{1,0:T(8,128)S(1)}, f32[16,256,64]{1,2,0:T(8,128)}) %tuple.46, (bf16[16,2,10,16,2,1024]{5,4,3,2,1,0:T(2,128)(2,1)}, s32[]{:T(128)}, ...), branch_computations={%region_2.2_spmd, %region_3.5_spmd} | conditional | flops 346562560 | bytes 46137424 | solution.py:90
  268.4 2.6 constant_dynamic-slice_fusion.1
  275.7 4.9 %fusion.7 = f32[16,256,64]{1,2,0:T(8,128)} fusion(f32[16,320,256]{2,1,0:T(8,128)} %copy-done.2, f32[16,256]{1,0:T(8,128)S(1)} %max.3, bf16[320,16,64]{2,1,0:T(8,128)(2,1)S(1)} %squeeze.25, f32[16,256,64]{1,2,0:T(8,128)} %get-tuple-element.163, f32[16,256]{1,0:T(8,128)S(1)} %get-tuple-element.243), kind=kOutput, calls=%fused_computation.8 | convolution fusion | flops 172228608 | bytes 8028160 | tf_op jit(solution)/shard_map/while/body/eval_jaxpr/cond/branch_1_fun/hqk,khd->hqd/dot_general | solution.py:79
  283.0 12.3 %conditional.2 = ((f32[16,256]{1,0:T(8,128)S(1)}, f32[16,256]{1,0:T(8,128)S(1)}, f32[16,256,64]{1,2,0:T(8,128)})) conditional(s32[]{:T(128)} %convert_element_type.63, (f32[16,256]{1,0:T(8,128)S(1)}, f32[16,256]{1,0:T(8,128)S(1)}, f32[16,256,64]{1,2,0:T(8,128)}) %tuple.46, (bf16[16,2,10,16,2,1024]{5,4,3,2,1,0:T(2,128)(2,1)}, s32[]{:T(128)}, ...), branch_computations={%region_2.2_spmd, %region_3.5_spmd} | conditional | flops 346562560 | bytes 46137424 | solution.py:90
  283.0 2.6 constant_dynamic-slice_fusion.1
  290.4 4.9 %fusion.7 = f32[16,256,64]{1,2,0:T(8,128)} fusion(f32[16,320,256]{2,1,0:T(8,128)} %copy-done.2, f32[16,256]{1,0:T(8,128)S(1)} %max.3, bf16[320,16,64]{2,1,0:T(8,128)(2,1)S(1)} %squeeze.25, f32[16,256,64]{1,2,0:T(8,128)} %get-tuple-element.163, f32[16,256]{1,0:T(8,128)S(1)} %get-tuple-element.243), kind=kOutput, calls=%fused_computation.8 | convolution fusion | flops 172228608 | bytes 8028160 | tf_op jit(solution)/shard_map/while/body/eval_jaxpr/cond/branch_1_fun/hqk,khd->hqd/dot_general | solution.py:79
  297.6 12.3 %conditional.2 = ((f32[16,256]{1,0:T(8,128)S(1)}, f32[16,256]{1,0:T(8,128)S(1)}, f32[16,256,64]{1,2,0:T(8,128)})) conditional(s32[]{:T(128)} %convert_element_type.63, (f32[16,256]{1,0:T(8,128)S(1)}, f32[16,256]{1,0:T(8,128)S(1)}, f32[16,256,64]{1,2,0:T(8,128)}) %tuple.46, (bf16[16,2,10,16,2,1024]{5,4,3,2,1,0:T(2,128)(2,1)}, s32[]{:T(128)}, ...), branch_computations={%region_2.2_spmd, %region_3.5_spmd} | conditional | flops 346562560 | bytes 46137424 | solution.py:90
  297.7 2.6 constant_dynamic-slice_fusion.1
  305.0 4.9 %fusion.7 = f32[16,256,64]{1,2,0:T(8,128)} fusion(f32[16,320,256]{2,1,0:T(8,128)} %copy-done.2, f32[16,256]{1,0:T(8,128)S(1)} %max.3, bf16[320,16,64]{2,1,0:T(8,128)(2,1)S(1)} %squeeze.25, f32[16,256,64]{1,2,0:T(8,128)} %get-tuple-element.163, f32[16,256]{1,0:T(8,128)S(1)} %get-tuple-element.243), kind=kOutput, calls=%fused_computation.8 | convolution fusion | flops 172228608 | bytes 8028160 | tf_op jit(solution)/shard_map/while/body/eval_jaxpr/cond/branch_1_fun/hqk,khd->hqd/dot_general | solution.py:79
  312.3 12.3 %conditional.2 = ((f32[16,256]{1,0:T(8,128)S(1)}, f32[16,256]{1,0:T(8,128)S(1)}, f32[16,256,64]{1,2,0:T(8,128)})) conditional(s32[]{:T(128)} %convert_element_type.63, (f32[16,256]{1,0:T(8,128)S(1)}, f32[16,256]{1,0:T(8,128)S(1)}, f32[16,256,64]{1,2,0:T(8,128)}) %tuple.46, (bf16[16,2,10,16,2,1024]{5,4,3,2,1,0:T(2,128)(2,1)}, s32[]{:T(128)}, ...), branch_computations={%region_2.2_spmd, %region_3.5_spmd} | conditional | flops 346562560 | bytes 46137424 | solution.py:90
  312.3 2.6 constant_dynamic-slice_fusion.1
  319.7 4.9 %fusion.7 = f32[16,256,64]{1,2,0:T(8,128)} fusion(f32[16,320,256]{2,1,0:T(8,128)} %copy-done.2, f32[16,256]{1,0:T(8,128)S(1)} %max.3, bf16[320,16,64]{2,1,0:T(8,128)(2,1)S(1)} %squeeze.25, f32[16,256,64]{1,2,0:T(8,128)} %get-tuple-element.163, f32[16,256]{1,0:T(8,128)S(1)} %get-tuple-element.243), kind=kOutput, calls=%fused_computation.8 | convolution fusion | flops 172228608 | bytes 8028160 | tf_op jit(solution)/shard_map/while/body/eval_jaxpr/cond/branch_1_fun/hqk,khd->hqd/dot_general | solution.py:79
  326.9 12.3 %conditional.2 = ((f32[16,256]{1,0:T(8,128)S(1)}, f32[16,256]{1,0:T(8,128)S(1)}, f32[16,256,64]{1,2,0:T(8,128)})) conditional(s32[]{:T(128)} %convert_element_type.63, (f32[16,256]{1,0:T(8,128)S(1)}, f32[16,256]{1,0:T(8,128)S(1)}, f32[16,256,64]{1,2,0:T(8,128)}) %tuple.46, (bf16[16,2,10,16,2,1024]{5,4,3,2,1,0:T(2,128)(2,1)}, s32[]{:T(128)}, ...), branch_computations={%region_2.2_spmd, %region_3.5_spmd} | conditional | flops 346562560 | bytes 46137424 | solution.py:90
  334.3 4.9 %fusion.7 = f32[16,256,64]{1,2,0:T(8,128)} fusion(f32[16,320,256]{2,1,0:T(8,128)} %copy-done.2, f32[16,256]{1,0:T(8,128)S(1)} %max.3, bf16[320,16,64]{2,1,0:T(8,128)(2,1)S(1)} %squeeze.25, f32[16,256,64]{1,2,0:T(8,128)} %get-tuple-element.163, f32[16,256]{1,0:T(8,128)S(1)} %get-tuple-element.243), kind=kOutput, calls=%fused_computation.8 | convolution fusion | flops 172228608 | bytes 8028160 | tf_op jit(solution)/shard_map/while/body/eval_jaxpr/cond/branch_1_fun/hqk,khd->hqd/dot_general | solution.py:79
  341.6 12.3 %conditional.2 = ((f32[16,256]{1,0:T(8,128)S(1)}, f32[16,256]{1,0:T(8,128)S(1)}, f32[16,256,64]{1,2,0:T(8,128)})) conditional(s32[]{:T(128)} %convert_element_type.63, (f32[16,256]{1,0:T(8,128)S(1)}, f32[16,256]{1,0:T(8,128)S(1)}, f32[16,256,64]{1,2,0:T(8,128)}) %tuple.46, (bf16[16,2,10,16,2,1024]{5,4,3,2,1,0:T(2,128)(2,1)}, s32[]{:T(128)}, ...), branch_computations={%region_2.2_spmd, %region_3.5_spmd} | conditional | flops 346562560 | bytes 46137424 | solution.py:90
  348.9 4.9 %fusion.7 = f32[16,256,64]{1,2,0:T(8,128)} fusion(f32[16,320,256]{2,1,0:T(8,128)} %copy-done.2, f32[16,256]{1,0:T(8,128)S(1)} %max.3, bf16[320,16,64]{2,1,0:T(8,128)(2,1)S(1)} %squeeze.25, f32[16,256,64]{1,2,0:T(8,128)} %get-tuple-element.163, f32[16,256]{1,0:T(8,128)S(1)} %get-tuple-element.243), kind=kOutput, calls=%fused_computation.8 | convolution fusion | flops 172228608 | bytes 8028160 | tf_op jit(solution)/shard_map/while/body/eval_jaxpr/cond/branch_1_fun/hqk,khd->hqd/dot_general | solution.py:79
  356.2 12.3 %conditional.2 = ((f32[16,256]{1,0:T(8,128)S(1)}, f32[16,256]{1,0:T(8,128)S(1)}, f32[16,256,64]{1,2,0:T(8,128)})) conditional(s32[]{:T(128)} %convert_element_type.63, (f32[16,256]{1,0:T(8,128)S(1)}, f32[16,256]{1,0:T(8,128)S(1)}, f32[16,256,64]{1,2,0:T(8,128)}) %tuple.46, (bf16[16,2,10,16,2,1024]{5,4,3,2,1,0:T(2,128)(2,1)}, s32[]{:T(128)}, ...), branch_computations={%region_2.2_spmd, %region_3.5_spmd} | conditional | flops 346562560 | bytes 46137424 | solution.py:90
  356.2 2.6 constant_dynamic-slice_fusion.1
  363.6 4.9 %fusion.7 = f32[16,256,64]{1,2,0:T(8,128)} fusion(f32[16,320,256]{2,1,0:T(8,128)} %copy-done.2, f32[16,256]{1,0:T(8,128)S(1)} %max.3, bf16[320,16,64]{2,1,0:T(8,128)(2,1)S(1)} %squeeze.25, f32[16,256,64]{1,2,0:T(8,128)} %get-tuple-element.163, f32[16,256]{1,0:T(8,128)S(1)} %get-tuple-element.243), kind=kOutput, calls=%fused_computation.8 | convolution fusion | flops 172228608 | bytes 8028160 | tf_op jit(solution)/shard_map/while/body/eval_jaxpr/cond/branch_1_fun/hqk,khd->hqd/dot_general | solution.py:79
  370.9 12.3 %conditional.2 = ((f32[16,256]{1,0:T(8,128)S(1)}, f32[16,256]{1,0:T(8,128)S(1)}, f32[16,256,64]{1,2,0:T(8,128)})) conditional(s32[]{:T(128)} %convert_element_type.63, (f32[16,256]{1,0:T(8,128)S(1)}, f32[16,256]{1,0:T(8,128)S(1)}, f32[16,256,64]{1,2,0:T(8,128)}) %tuple.46, (bf16[16,2,10,16,2,1024]{5,4,3,2,1,0:T(2,128)(2,1)}, s32[]{:T(128)}, ...), branch_computations={%region_2.2_spmd, %region_3.5_spmd} | conditional | flops 346562560 | bytes 46137424 | solution.py:90
  378.2 4.9 %fusion.7 = f32[16,256,64]{1,2,0:T(8,128)} fusion(f32[16,320,256]{2,1,0:T(8,128)} %copy-done.2, f32[16,256]{1,0:T(8,128)S(1)} %max.3, bf16[320,16,64]{2,1,0:T(8,128)(2,1)S(1)} %squeeze.25, f32[16,256,64]{1,2,0:T(8,128)} %get-tuple-element.163, f32[16,256]{1,0:T(8,128)S(1)} %get-tuple-element.243), kind=kOutput, calls=%fused_computation.8 | convolution fusion | flops 172228608 | bytes 8028160 | tf_op jit(solution)/shard_map/while/body/eval_jaxpr/cond/branch_1_fun/hqk,khd->hqd/dot_general | solution.py:79
  385.5 12.3 %conditional.2 = ((f32[16,256]{1,0:T(8,128)S(1)}, f32[16,256]{1,0:T(8,128)S(1)}, f32[16,256,64]{1,2,0:T(8,128)})) conditional(s32[]{:T(128)} %convert_element_type.63, (f32[16,256]{1,0:T(8,128)S(1)}, f32[16,256]{1,0:T(8,128)S(1)}, f32[16,256,64]{1,2,0:T(8,128)}) %tuple.46, (bf16[16,2,10,16,2,1024]{5,4,3,2,1,0:T(2,128)(2,1)}, s32[]{:T(128)}, ...), branch_computations={%region_2.2_spmd, %region_3.5_spmd} | conditional | flops 346562560 | bytes 46137424 | solution.py:90
  385.5 2.6 constant_dynamic-slice_fusion.1
  392.9 4.9 %fusion.7 = f32[16,256,64]{1,2,0:T(8,128)} fusion(f32[16,320,256]{2,1,0:T(8,128)} %copy-done.2, f32[16,256]{1,0:T(8,128)S(1)} %max.3, bf16[320,16,64]{2,1,0:T(8,128)(2,1)S(1)} %squeeze.25, f32[16,256,64]{1,2,0:T(8,128)} %get-tuple-element.163, f32[16,256]{1,0:T(8,128)S(1)} %get-tuple-element.243), kind=kOutput, calls=%fused_computation.8 | convolution fusion | flops 172228608 | bytes 8028160 | tf_op jit(solution)/shard_map/while/body/eval_jaxpr/cond/branch_1_fun/hqk,khd->hqd/dot_general | solution.py:79
  400.2 12.3 %conditional.2 = ((f32[16,256]{1,0:T(8,128)S(1)}, f32[16,256]{1,0:T(8,128)S(1)}, f32[16,256,64]{1,2,0:T(8,128)})) conditional(s32[]{:T(128)} %convert_element_type.63, (f32[16,256]{1,0:T(8,128)S(1)}, f32[16,256]{1,0:T(8,128)S(1)}, f32[16,256,64]{1,2,0:T(8,128)}) %tuple.46, (bf16[16,2,10,16,2,1024]{5,4,3,2,1,0:T(2,128)(2,1)}, s32[]{:T(128)}, ...), branch_computations={%region_2.2_spmd, %region_3.5_spmd} | conditional | flops 346562560 | bytes 46137424 | solution.py:90
  407.5 4.9 %fusion.7 = f32[16,256,64]{1,2,0:T(8,128)} fusion(f32[16,320,256]{2,1,0:T(8,128)} %copy-done.2, f32[16,256]{1,0:T(8,128)S(1)} %max.3, bf16[320,16,64]{2,1,0:T(8,128)(2,1)S(1)} %squeeze.25, f32[16,256,64]{1,2,0:T(8,128)} %get-tuple-element.163, f32[16,256]{1,0:T(8,128)S(1)} %get-tuple-element.243), kind=kOutput, calls=%fused_computation.8 | convolution fusion | flops 172228608 | bytes 8028160 | tf_op jit(solution)/shard_map/while/body/eval_jaxpr/cond/branch_1_fun/hqk,khd->hqd/dot_general | solution.py:79
  414.8 12.3 %conditional.2 = ((f32[16,256]{1,0:T(8,128)S(1)}, f32[16,256]{1,0:T(8,128)S(1)}, f32[16,256,64]{1,2,0:T(8,128)})) conditional(s32[]{:T(128)} %convert_element_type.63, (f32[16,256]{1,0:T(8,128)S(1)}, f32[16,256]{1,0:T(8,128)S(1)}, f32[16,256,64]{1,2,0:T(8,128)}) %tuple.46, (bf16[16,2,10,16,2,1024]{5,4,3,2,1,0:T(2,128)(2,1)}, s32[]{:T(128)}, ...), branch_computations={%region_2.2_spmd, %region_3.5_spmd} | conditional | flops 346562560 | bytes 46137424 | solution.py:90
  414.8 2.6 constant_dynamic-slice_fusion.1
  422.2 4.9 %fusion.7 = f32[16,256,64]{1,2,0:T(8,128)} fusion(f32[16,320,256]{2,1,0:T(8,128)} %copy-done.2, f32[16,256]{1,0:T(8,128)S(1)} %max.3, bf16[320,16,64]{2,1,0:T(8,128)(2,1)S(1)} %squeeze.25, f32[16,256,64]{1,2,0:T(8,128)} %get-tuple-element.163, f32[16,256]{1,0:T(8,128)S(1)} %get-tuple-element.243), kind=kOutput, calls=%fused_computation.8 | convolution fusion | flops 172228608 | bytes 8028160 | tf_op jit(solution)/shard_map/while/body/eval_jaxpr/cond/branch_1_fun/hqk,khd->hqd/dot_general | solution.py:79
  429.4 12.3 %conditional.2 = ((f32[16,256]{1,0:T(8,128)S(1)}, f32[16,256]{1,0:T(8,128)S(1)}, f32[16,256,64]{1,2,0:T(8,128)})) conditional(s32[]{:T(128)} %convert_element_type.63, (f32[16,256]{1,0:T(8,128)S(1)}, f32[16,256]{1,0:T(8,128)S(1)}, f32[16,256,64]{1,2,0:T(8,128)}) %tuple.46, (bf16[16,2,10,16,2,1024]{5,4,3,2,1,0:T(2,128)(2,1)}, s32[]{:T(128)}, ...), branch_computations={%region_2.2_spmd, %region_3.5_spmd} | conditional | flops 346562560 | bytes 46137424 | solution.py:90
  436.8 4.9 %fusion.7 = f32[16,256,64]{1,2,0:T(8,128)} fusion(f32[16,320,256]{2,1,0:T(8,128)} %copy-done.2, f32[16,256]{1,0:T(8,128)S(1)} %max.3, bf16[320,16,64]{2,1,0:T(8,128)(2,1)S(1)} %squeeze.25, f32[16,256,64]{1,2,0:T(8,128)} %get-tuple-element.163, f32[16,256]{1,0:T(8,128)S(1)} %get-tuple-element.243), kind=kOutput, calls=%fused_computation.8 | convolution fusion | flops 172228608 | bytes 8028160 | tf_op jit(solution)/shard_map/while/body/eval_jaxpr/cond/branch_1_fun/hqk,khd->hqd/dot_general | solution.py:79
  (212 shorter events, 122.1 us)
Async XLA Ops:
  6.5 4.6 %copy-start = (bf16[1024,1024]{1,0:T(8,128)(2,1)S(1)}, bf16[1024,1024]{1,0:T(8,128)(2,1)}, u32[]{:S(2)}) copy-start(bf16[1024,1024]{1,0:T(8,128)(2,1)} %param.15) | copy-start | bytes 6291460
  6.5 161.3 %all-gather.2.cloned.1.call-start = ((), (), s32[]{:S(2)}) async-start(), calls=%async_computation | async-start | bytes 22282240 | tf_op jit(solution)/shard_map/all_gather | solution.py:98
  14.9 12.6 %collective-permute-start = (bf16[2,2,16,2,1024]{4,2,3,1,0:T(8,128)(2,1)S(1)}, bf16[2,2,16,2,1024]{4,2,3,1,0:T(8,128)(2,1)S(1)}, u32[]{:S(2)}, u32[]{:S(2)}) collective-permute-start(bf16[2,2,16,2,1024]{4,2,3,1,0:T(8,128)(2,1)S(1)} %pad_maximum_fusion.1), channel_id=1, source_target_pairs={{0,8},{1,9},{2,10},{3,11},{4,12},{5,13},{6,14},{7,15},{8,0},{9,1},... | collective-permute-start | bytes 786440 | tf_op jit(solution)/shard_map/ppermute | solution.py:25
  18.6 7.8 %collective-permute-start.1 = (bf16[2,1,16,2,1024]{4,2,3,1,0:T(8,128)(2,1)S(1)}, bf16[2,1,16,2,1024]{4,2,3,1,0:T(8,128)(2,1)S(1)}, u32[]{:S(2)}, u32[]{:S(2)}) collective-permute-start(bf16[2,1,16,2,1024]{4,2,3,1,0:T(8,128)(2,1)S(1)} %get-tuple-element.248), channel_id=1, source_target_pairs={{0,16},{16,32},{32,48},{48,64},{64,80},{80,96},{96,112},{112,128},... | collective-permute-start | bytes 393224 | tf_op jit(solution)/shard_map/ppermute | solution.py:16
  20.8 6.8 %collective-permute-start.2 = (bf16[2,1,16,2,1024]{4,2,3,1,0:T(8,128)(2,1)S(1)}, bf16[2,1,16,2,1024]{4,2,3,1,0:T(8,128)(2,1)S(1)}, u32[]{:S(2)}, u32[]{:S(2)}) collective-permute-start(bf16[2,1,16,2,1024]{4,2,3,1,0:T(8,128)(2,1)S(1)} %get-tuple-element.249), channel_id=1, source_target_pairs={{16,0},{32,16},{48,32},{64,48},{80,64},{96,80},{112,96},{128,112},... | collective-permute-start | bytes 393224 | tf_op jit(solution)/shard_map/ppermute | solution.py:17
  27.6 1.3 copy-start.3
  28.8 1.2 copy-start.5
  28.8 1.8 copy-start.6
  214.0 2.3 copy-start.2
  228.7 2.3 copy-start.2
  243.3 2.3 copy-start.2
  258.0 2.3 copy-start.2
  272.6 2.3 copy-start.2
  287.2 2.3 copy-start.2
  301.9 2.3 copy-start.2
  316.5 2.3 copy-start.2
  331.2 2.3 copy-start.2
  345.8 2.3 copy-start.2
  360.5 2.3 copy-start.2
  375.1 2.3 copy-start.2
  389.8 2.3 copy-start.2
  404.4 2.3 copy-start.2
  419.0 2.3 copy-start.2
  433.7 2.3 copy-start.2
  441.7 1.5 copy-start.4
  443.2 3.6 copy-start.1
Sparse Core Ops, SparseCore 0:
  29.0 138.8 all-gather.1
where the time goes:
time: 455 us; the launch traced here: 454 us
  local copies, waits for them, and re-layouts  142 us (31%)
  waiting for transfers between devices  139 us (31%)
  matrix products  99.8 us (22%)
  loops' own time  30 us (7%)
  other arithmetic  21.2 us (5%)
  between operations  13.6 us (3%)
  starting transfers between devices  7.33 us (2%)
    all_gather x1, waiting for transfers between devices, body(): piece = lax.all_gather(extended, 'lon', axis=2, tiled=True)  134 us
    dot_general x16, matrix products, update(): jnp.einsum('hqk,khd->hqd', raw.astype(jnp.bfloat16), value_heads, preferr...  78.7 us
    slice x16, local copies, waits for them, and re-layouts, update(): value_heads = piece[1].reshape(-1, heads, HD)  41.9 us
    while x1, local copies, waits for them, and re-layouts, body(): lax.scan(advance, carry, (split, jnp.arange(count, dtype=jnp.int32)))  38.5 us
    another operation x1, loops' own time, body(): lax.scan(advance, carry, (split, jnp.arange(count, dtype=jnp.int32)))  28.8 us
    cond x48, local copies, waits for them, and re-layouts  23.1 us
    reduce_sum x16, other arithmetic, update(): total = total * fade + jnp.sum(raw, -1)  14.1 us
    dot_general x16, matrix products, update(): jnp.einsum('qhd,khd->hqk', query_heads, key_heads, preferred_element_type...  13.4 us
  transfers between devices with their start and end apart: 4, of which 3 were waited for; matrix products, arithmetic and copies ran while one was open for 1% of the time, Pallas kernels for 0%

commit v1 on v0

--- a/solution.py
+++ b/solution.py
@@ -95,7 +95,10 @@
         jnp.zeros((heads, count_queries, HD), jnp.float32),
     )
     carry = initial
-    piece = lax.all_gather(extended, "lon", axis=2, tiled=True)
+    size = lax.axis_size("lon")
+    blocks = jnp.stack([extended for _ in range(size)])
+    blocks = lax.all_to_all(blocks, "lon", split_axis=0, concat_axis=0)
+    piece = jnp.concatenate(blocks, axis=2)
     count = piece.shape[2] // columns
     split = jnp.moveaxis(piece.reshape(2, rows + 2, count, columns, levels, width), 2, 0)
 

time: 455 us -> 623 us (1.37); the launches traced: 454 us -> 613 us
  waiting for transfers between devices: 139 us -> 320 us
  local copies, waits for them, and re-layouts: 142 us -> 124 us
  between operations: 13.6 us -> 0.17 us
  starting transfers between devices: 7.33 us -> 15.6 us
    all_to_all x0 -> x1, waiting for transfers between devices: none -> 314 us  [body(): blocks = lax.all_to_all(blocks, 'lon', split_axis=0, concat_axis=0)]
    all_gather x1 -> x0, waiting for transfers between devices: 134 us -> none  [body(): piece = lax.all_gather(extended, 'lon', axis=2, tiled=True)]
    while x1 -> x0, local copies, waits for them, and re-layouts: 38.5 us -> none  [body(): lax.scan(advance, carry, (split, jnp.arange(count, dtype=jnp.int32)))]
    another operation x0 -> x1, local copies, waits for them, and re-layouts: none -> 17.9 us  [body(): blocks = jnp.stack([extended for _ in range(size)])]
    all_to_all x0 -> x1, starting transfers between devices: none -> 8.42 us  [body(): blocks = lax.all_to_all(blocks, 'lon', split_axis=0, concat_axis=0)]
where the time goes in v1:
time: 623 us; the launch traced here: 613 us
  waiting for transfers between devices  320 us (51%)
  local copies, waits for them, and re-layouts  124 us (20%)
  matrix products  99.9 us (16%)
  loops' own time  31.1 us (5%)
  other arithmetic  22.6 us (4%)
  starting transfers between devices  15.6 us (3%)
    all_to_all x1, waiting for transfers between devices, body(): blocks = lax.all_to_all(blocks, 'lon', split_axis=0, concat_axis=0)  314 us
    dot_general x16, matrix products, update(): jnp.einsum('hqk,khd->hqd', raw.astype(jnp.bfloat16), value_heads, preferr...  78.8 us
    slice x16, local copies, waits for them, and re-layouts, update(): value_heads = piece[1].reshape(-1, heads, HD)  41.9 us
    another operation x1, loops' own time, body(): lax.scan(advance, carry, (split, jnp.arange(count, dtype=jnp.int32)))  29.9 us
    cond x48, local copies, waits for them, and re-layouts  22.9 us
    another operation x1, local copies, waits for them, and re-layouts, body(): blocks = jnp.stack([extended for _ in range(size)])  17.9 us
    reduce_sum x16, other arithmetic, update(): total = total * fade + jnp.sum(raw, -1)  14.1 us
    dot_general x16, matrix products, update(): jnp.einsum('qhd,khd->hqk', query_heads, key_heads, preferred_element_type...  13.4 us
  transfers between devices with their start and end apart: 4, of which 3 were waited for; matrix products, arithmetic and copies ran while one was open for 1% of the time, Pallas kernels for 0%

profile of v1, /device:TPU:1, one launch (start us, length us, event | category | flops | bytes accessed | tf_op | source)
XLA Modules:
  0.0 612.7 jit_solution(11068890220083350508)
XLA Ops:
  9.4 3.6 collective-permute-start
  16.6 4.3 collective-permute-done.1
  24.3 17.9 %stack.8 = bf16[16,2,10,16,2,1024]{5,4,3,2,1,0:T(2,128)(2,1)} broadcast(bf16[2,10,16,2,1024]{4,3,2,1,0:T(2,128)(2,1)S(1)} %pad_maximum_fusion), dimensions={1,2,3,4,5} | broadcast | bytes 22282240 | tf_op jit(solution)/shard_map/stack | solution.py:99
  42.3 8.4 %all-to-all-start = ((bf16[16,2,10,16,2,1024]{5,4,3,2,1,0:T(2,128)(2,1)}), bf16[16,2,10,16,2,1024]{5,4,3,2,1,0:T(2,128)(2,1)}, u32[]{:S(2)}, u32[]{:S(2)}) async-start(bf16[16,2,10,16,2,1024]{5,4,3,2,1,0:T(2,128)(2,1)} %stack.8), calls=%async_computation | async-start | bytes 41943040 | tf_op jit(solution)/shard_map/all_to_all | solution.py:100
  55.6 314.3 %all-to-all-done = bf16[16,2,10,16,2,1024]{5,4,3,2,1,0:T(2,128)(2,1)} async-done(((bf16[16,2,10,16,2,1024]{5,4,3,2,1,0:T(2,128)(2,1)}), bf16[16,2,10,16,2,1024]{5,4,3,2,1,0:T(2,128)(2,1)}, u32[]{:S(2)}, u32[]{:S(2)}) %all-to-all-start) | async-done | bytes 20971552 | tf_op jit(solution)/shard_map/all_to_all | solution.py:100
  370.9 236.8 %while.16 = (s32[]{:T(128)}, f32[16,256]{1,0:T(8,128)S(1)}, f32[16,256]{1,0:T(8,128)S(1)}, f32[16,256,64]{1,2,0:T(8,128)}, s32[16]{0:T(128)S(1)}, /*index=5*/s32...) while((s32[]{:T(128)}, f32[16,256]{1,0:T(8,128)S(1)}, ...), condition=%wide.region_6.7_spmd, body=%wide.region_1.6_spmd.sunk | while | flops 346562560 | bytes 46137788 | solution.py:109
  373.5 12.3 %conditional.2 = ((f32[16,256]{1,0:T(8,128)S(1)}, f32[16,256]{1,0:T(8,128)S(1)}, f32[16,256,64]{1,2,0:T(8,128)})) conditional(s32[]{:T(128)} %convert_element_type.63, (f32[16,256]{1,0:T(8,128)S(1)}, f32[16,256]{1,0:T(8,128)S(1)}, f32[16,256,64]{1,2,0:T(8,128)}) %tuple.43, (bf16[16,2,10,16,2,1024]{5,4,3,2,1,0:T(2,128)(2,1)}, s32[]{:T(128)}, ...), branch_computations={%region_2.2_spmd, %region_3.5_spmd} | conditional | flops 346562560 | bytes 46137424 | solution.py:90
  373.5 2.6 constant_dynamic-slice_fusion.1
  380.8 4.9 fusion.7
  388.3 12.3 %conditional.2 = ((f32[16,256]{1,0:T(8,128)S(1)}, f32[16,256]{1,0:T(8,128)S(1)}, f32[16,256,64]{1,2,0:T(8,128)})) conditional(s32[]{:T(128)} %convert_element_type.63, (f32[16,256]{1,0:T(8,128)S(1)}, f32[16,256]{1,0:T(8,128)S(1)}, f32[16,256,64]{1,2,0:T(8,128)}) %tuple.43, (bf16[16,2,10,16,2,1024]{5,4,3,2,1,0:T(2,128)(2,1)}, s32[]{:T(128)}, ...), branch_computations={%region_2.2_spmd, %region_3.5_spmd} | conditional | flops 346562560 | bytes 46137424 | solution.py:90
  388.3 2.6 constant_dynamic-slice_fusion.1
  395.6 4.9 fusion.7
  403.1 12.3 %conditional.2 = ((f32[16,256]{1,0:T(8,128)S(1)}, f32[16,256]{1,0:T(8,128)S(1)}, f32[16,256,64]{1,2,0:T(8,128)})) conditional(s32[]{:T(128)} %convert_element_type.63, (f32[16,256]{1,0:T(8,128)S(1)}, f32[16,256]{1,0:T(8,128)S(1)}, f32[16,256,64]{1,2,0:T(8,128)}) %tuple.43, (bf16[16,2,10,16,2,1024]{5,4,3,2,1,0:T(2,128)(2,1)}, s32[]{:T(128)}, ...), branch_computations={%region_2.2_spmd, %region_3.5_spmd} | conditional | flops 346562560 | bytes 46137424 | solution.py:90
  403.1 2.6 constant_dynamic-slice_fusion.1
  410.4 4.9 fusion.7
  417.9 12.3 %conditional.2 = ((f32[16,256]{1,0:T(8,128)S(1)}, f32[16,256]{1,0:T(8,128)S(1)}, f32[16,256,64]{1,2,0:T(8,128)})) conditional(s32[]{:T(128)} %convert_element_type.63, (f32[16,256]{1,0:T(8,128)S(1)}, f32[16,256]{1,0:T(8,128)S(1)}, f32[16,256,64]{1,2,0:T(8,128)}) %tuple.43, (bf16[16,2,10,16,2,1024]{5,4,3,2,1,0:T(2,128)(2,1)}, s32[]{:T(128)}, ...), branch_computations={%region_2.2_spmd, %region_3.5_spmd} | conditional | flops 346562560 | bytes 46137424 | solution.py:90
  417.9 2.6 constant_dynamic-slice_fusion.1
  425.2 4.9 fusion.7
  432.7 12.3 %conditional.2 = ((f32[16,256]{1,0:T(8,128)S(1)}, f32[16,256]{1,0:T(8,128)S(1)}, f32[16,256,64]{1,2,0:T(8,128)})) conditional(s32[]{:T(128)} %convert_element_type.63, (f32[16,256]{1,0:T(8,128)S(1)}, f32[16,256]{1,0:T(8,128)S(1)}, f32[16,256,64]{1,2,0:T(8,128)}) %tuple.43, (bf16[16,2,10,16,2,1024]{5,4,3,2,1,0:T(2,128)(2,1)}, s32[]{:T(128)}, ...), branch_computations={%region_2.2_spmd, %region_3.5_spmd} | conditional | flops 346562560 | bytes 46137424 | solution.py:90
  432.7 2.6 constant_dynamic-slice_fusion.1
  440.0 4.9 fusion.7
  447.5 12.3 %conditional.2 = ((f32[16,256]{1,0:T(8,128)S(1)}, f32[16,256]{1,0:T(8,128)S(1)}, f32[16,256,64]{1,2,0:T(8,128)})) conditional(s32[]{:T(128)} %convert_element_type.63, (f32[16,256]{1,0:T(8,128)S(1)}, f32[16,256]{1,0:T(8,128)S(1)}, f32[16,256,64]{1,2,0:T(8,128)}) %tuple.43, (bf16[16,2,10,16,2,1024]{5,4,3,2,1,0:T(2,128)(2,1)}, s32[]{:T(128)}, ...), branch_computations={%region_2.2_spmd, %region_3.5_spmd} | conditional | flops 346562560 | bytes 46137424 | solution.py:90
  447.5 2.6 constant_dynamic-slice_fusion.1
  454.8 4.9 fusion.7
  462.3 12.3 %conditional.2 = ((f32[16,256]{1,0:T(8,128)S(1)}, f32[16,256]{1,0:T(8,128)S(1)}, f32[16,256,64]{1,2,0:T(8,128)})) conditional(s32[]{:T(128)} %convert_element_type.63, (f32[16,256]{1,0:T(8,128)S(1)}, f32[16,256]{1,0:T(8,128)S(1)}, f32[16,256,64]{1,2,0:T(8,128)}) %tuple.43, (bf16[16,2,10,16,2,1024]{5,4,3,2,1,0:T(2,128)(2,1)}, s32[]{:T(128)}, ...), branch_computations={%region_2.2_spmd, %region_3.5_spmd} | conditional | flops 346562560 | bytes 46137424 | solution.py:90
  462.3 2.6 constant_dynamic-slice_fusion.1
  469.6 4.9 fusion.7
  477.1 12.3 %conditional.2 = ((f32[16,256]{1,0:T(8,128)S(1)}, f32[16,256]{1,0:T(8,128)S(1)}, f32[16,256,64]{1,2,0:T(8,128)})) conditional(s32[]{:T(128)} %convert_element_type.63, (f32[16,256]{1,0:T(8,128)S(1)}, f32[16,256]{1,0:T(8,128)S(1)}, f32[16,256,64]{1,2,0:T(8,128)}) %tuple.43, (bf16[16,2,10,16,2,1024]{5,4,3,2,1,0:T(2,128)(2,1)}, s32[]{:T(128)}, ...), branch_computations={%region_2.2_spmd, %region_3.5_spmd} | conditional | flops 346562560 | bytes 46137424 | solution.py:90
  477.1 2.6 constant_dynamic-slice_fusion.1
  484.4 4.9 fusion.7
  491.9 12.3 %conditional.2 = ((f32[16,256]{1,0:T(8,128)S(1)}, f32[16,256]{1,0:T(8,128)S(1)}, f32[16,256,64]{1,2,0:T(8,128)})) conditional(s32[]{:T(128)} %convert_element_type.63, (f32[16,256]{1,0:T(8,128)S(1)}, f32[16,256]{1,0:T(8,128)S(1)}, f32[16,256,64]{1,2,0:T(8,128)}) %tuple.43, (bf16[16,2,10,16,2,1024]{5,4,3,2,1,0:T(2,128)(2,1)}, s32[]{:T(128)}, ...), branch_computations={%region_2.2_spmd, %region_3.5_spmd} | conditional | flops 346562560 | bytes 46137424 | solution.py:90
  491.9 2.6 constant_dynamic-slice_fusion.1
  499.2 4.9 fusion.7
  506.7 12.3 %conditional.2 = ((f32[16,256]{1,0:T(8,128)S(1)}, f32[16,256]{1,0:T(8,128)S(1)}, f32[16,256,64]{1,2,0:T(8,128)})) conditional(s32[]{:T(128)} %convert_element_type.63, (f32[16,256]{1,0:T(8,128)S(1)}, f32[16,256]{1,0:T(8,128)S(1)}, f32[16,256,64]{1,2,0:T(8,128)}) %tuple.43, (bf16[16,2,10,16,2,1024]{5,4,3,2,1,0:T(2,128)(2,1)}, s32[]{:T(128)}, ...), branch_computations={%region_2.2_spmd, %region_3.5_spmd} | conditional | flops 346562560 | bytes 46137424 | solution.py:90
  506.7 2.6 constant_dynamic-slice_fusion.1
  514.0 4.9 fusion.7
  521.5 12.3 %conditional.2 = ((f32[16,256]{1,0:T(8,128)S(1)}, f32[16,256]{1,0:T(8,128)S(1)}, f32[16,256,64]{1,2,0:T(8,128)})) conditional(s32[]{:T(128)} %convert_element_type.63, (f32[16,256]{1,0:T(8,128)S(1)}, f32[16,256]{1,0:T(8,128)S(1)}, f32[16,256,64]{1,2,0:T(8,128)}) %tuple.43, (bf16[16,2,10,16,2,1024]{5,4,3,2,1,0:T(2,128)(2,1)}, s32[]{:T(128)}, ...), branch_computations={%region_2.2_spmd, %region_3.5_spmd} | conditional | flops 346562560 | bytes 46137424 | solution.py:90
  528.8 4.9 fusion.7
  536.3 12.3 %conditional.2 = ((f32[16,256]{1,0:T(8,128)S(1)}, f32[16,256]{1,0:T(8,128)S(1)}, f32[16,256,64]{1,2,0:T(8,128)})) conditional(s32[]{:T(128)} %convert_element_type.63, (f32[16,256]{1,0:T(8,128)S(1)}, f32[16,256]{1,0:T(8,128)S(1)}, f32[16,256,64]{1,2,0:T(8,128)}) %tuple.43, (bf16[16,2,10,16,2,1024]{5,4,3,2,1,0:T(2,128)(2,1)}, s32[]{:T(128)}, ...), branch_computations={%region_2.2_spmd, %region_3.5_spmd} | conditional | flops 346562560 | bytes 46137424 | solution.py:90
  543.6 4.9 fusion.7
  551.1 12.3 %conditional.2 = ((f32[16,256]{1,0:T(8,128)S(1)}, f32[16,256]{1,0:T(8,128)S(1)}, f32[16,256,64]{1,2,0:T(8,128)})) conditional(s32[]{:T(128)} %convert_element_type.63, (f32[16,256]{1,0:T(8,128)S(1)}, f32[16,256]{1,0:T(8,128)S(1)}, f32[16,256,64]{1,2,0:T(8,128)}) %tuple.43, (bf16[16,2,10,16,2,1024]{5,4,3,2,1,0:T(2,128)(2,1)}, s32[]{:T(128)}, ...), branch_computations={%region_2.2_spmd, %region_3.5_spmd} | conditional | flops 346562560 | bytes 46137424 | solution.py:90
  558.4 4.9 fusion.7
  565.9 12.3 %conditional.2 = ((f32[16,256]{1,0:T(8,128)S(1)}, f32[16,256]{1,0:T(8,128)S(1)}, f32[16,256,64]{1,2,0:T(8,128)})) conditional(s32[]{:T(128)} %convert_element_type.63, (f32[16,256]{1,0:T(8,128)S(1)}, f32[16,256]{1,0:T(8,128)S(1)}, f32[16,256,64]{1,2,0:T(8,128)}) %tuple.43, (bf16[16,2,10,16,2,1024]{5,4,3,2,1,0:T(2,128)(2,1)}, s32[]{:T(128)}, ...), branch_computations={%region_2.2_spmd, %region_3.5_spmd} | conditional | flops 346562560 | bytes 46137424 | solution.py:90
  573.2 4.9 fusion.7
  580.7 12.3 %conditional.2 = ((f32[16,256]{1,0:T(8,128)S(1)}, f32[16,256]{1,0:T(8,128)S(1)}, f32[16,256,64]{1,2,0:T(8,128)})) conditional(s32[]{:T(128)} %convert_element_type.63, (f32[16,256]{1,0:T(8,128)S(1)}, f32[16,256]{1,0:T(8,128)S(1)}, f32[16,256,64]{1,2,0:T(8,128)}) %tuple.43, (bf16[16,2,10,16,2,1024]{5,4,3,2,1,0:T(2,128)(2,1)}, s32[]{:T(128)}, ...), branch_computations={%region_2.2_spmd, %region_3.5_spmd} | conditional | flops 346562560 | bytes 46137424 | solution.py:90
  588.0 4.9 fusion.7
  595.5 12.3 %conditional.2 = ((f32[16,256]{1,0:T(8,128)S(1)}, f32[16,256]{1,0:T(8,128)S(1)}, f32[16,256,64]{1,2,0:T(8,128)})) conditional(s32[]{:T(128)} %convert_element_type.63, (f32[16,256]{1,0:T(8,128)S(1)}, f32[16,256]{1,0:T(8,128)S(1)}, f32[16,256,64]{1,2,0:T(8,128)}) %tuple.43, (bf16[16,2,10,16,2,1024]{5,4,3,2,1,0:T(2,128)(2,1)}, s32[]{:T(128)}, ...), branch_computations={%region_2.2_spmd, %region_3.5_spmd} | conditional | flops 346562560 | bytes 46137424 | solution.py:90
  602.8 4.9 fusion.7
  (211 shorter events, 127.9 us)
Async XLA Ops:
  0.0 4.6 copy-start
  9.4 12.6 %collective-permute-start = (bf16[2,2,16,2,1024]{4,3,2,1,0:T(2,128)(2,1)S(1)}, bf16[2,2,16,2,1024]{4,3,2,1,0:T(2,128)(2,1)S(1)}, u32[]{:S(2)}, u32[]{:S(2)}) collective-permute-start(bf16[2,2,16,2,1024]{4,3,2,1,0:T(2,128)(2,1)S(1)} %pad_maximum_fusion.1), channel_id=1, source_target_pairs={{0,8},{1,9},{2,10},{3,11},{4,12},{5,13},{6,14},{7,15},{8,0},{9,1},... | collective-permute-start | bytes 786440 | tf_op jit(solution)/shard_map/ppermute | solution.py:25
  13.0 7.8 %collective-permute-start.1 = (bf16[2,1,16,2,1024]{4,3,2,1,0:T(2,128)(2,1)S(1)}, bf16[2,1,16,2,1024]{4,3,2,1,0:T(2,128)(2,1)S(1)}, u32[]{:S(2)}, u32[]{:S(2)}) collective-permute-start(bf16[2,1,16,2,1024]{4,3,2,1,0:T(2,128)(2,1)S(1)} %get-tuple-element.218), channel_id=1, source_target_pairs={{0,16},{16,32},{32,48},{48,64},{64,80},{80,96},{96,112},{112,128},... | collective-permute-start | bytes 393224 | tf_op jit(solution)/shard_map/ppermute | solution.py:16
  15.3 6.8 %collective-permute-start.2 = (bf16[2,1,16,2,1024]{4,3,2,1,0:T(2,128)(2,1)S(1)}, bf16[2,1,16,2,1024]{4,3,2,1,0:T(2,128)(2,1)S(1)}, u32[]{:S(2)}, u32[]{:S(2)}) collective-permute-start(bf16[2,1,16,2,1024]{4,3,2,1,0:T(2,128)(2,1)S(1)} %get-tuple-element.219), channel_id=1, source_target_pairs={{16,0},{32,16},{48,32},{64,48},{80,64},{96,80},{112,96},{128,112},... | collective-permute-start | bytes 393224 | tf_op jit(solution)/shard_map/ppermute | solution.py:17
  42.3 8.4 %copy-start.3 = (bf16[8,16,2,1024]{3,2,1,0:T(2,128)(2,1)S(1)}, bf16[8,16,2,1024]{3,2,1,0:T(2,128)(2,1)}, u32[]{:S(2)}) copy-start(bf16[8,16,2,1024]{3,2,1,0:T(2,128)(2,1)} %param.12) | copy-start | bytes 1572868
  42.3 9.6 %copy-start.5 = (s32[16]{0:T(128)S(1)}, s32[16]{0:T(128)}, u32[]{:S(2)}) copy-start(s32[16]{0:T(128)} %param.18) | copy-start | bytes 196
  42.3 10.2 %copy-start.6 = (s32[16]{0:T(128)S(1)}, s32[16]{0:T(128)}, u32[]{:S(2)}) copy-start(s32[16]{0:T(128)} %param.19) | copy-start | bytes 196
  42.3 327.6 %all-to-all-start = ((bf16[16,2,10,16,2,1024]{5,4,3,2,1,0:T(2,128)(2,1)}), bf16[16,2,10,16,2,1024]{5,4,3,2,1,0:T(2,128)(2,1)}, u32[]{:S(2)}, u32[]{:S(2)}) async-start(bf16[16,2,10,16,2,1024]{5,4,3,2,1,0:T(2,128)(2,1)} %stack.8), calls=%async_computation | async-start | bytes 41943040 | tf_op jit(solution)/shard_map/all_to_all | solution.py:100
  377.7 2.3 copy-start.2
  392.5 2.3 copy-start.2
  407.3 2.3 copy-start.2
  422.1 2.3 copy-start.2
  436.9 2.3 copy-start.2
  451.7 2.3 copy-start.2
  466.5 2.3 copy-start.2
  481.3 2.3 copy-start.2
  496.1 2.3 copy-start.2
  510.9 2.3 copy-start.2
  525.7 2.3 copy-start.2
  540.5 2.3 copy-start.2
  555.3 2.3 copy-start.2
  570.1 2.3 copy-start.2
  584.9 2.3 copy-start.2
  599.7 2.3 copy-start.2
  607.7 1.5 copy-start.4
  609.2 3.6 copy-start.1
